TPU v7x, 512 devices: a whole 4x8x8 slice. The times are simulated.
512 devices in a mesh: gy: 32 (over x, y_hi, core), gz: 16 (over y_lo, z).
Axes of the slice: x: 4, y: 8 (y_hi: 4, y_lo: 2; y = y_hi * 2 + y_lo), z: 8, core: 2. Of those that a mesh axis runs over, the one named last changes fastest.
Arguments:
- ckpt_pops: float32 [27, 64, 128, 128], P(None, 'gy', 'gz'), may hold values from 0 to 1, as said below
- adjoint_pops: float32 [27, 64, 128, 128], P(None, 'gy', 'gz'), may hold values from -8 to 8
- design: float32 [64, 128, 128], P('gy', 'gz'), may hold values from 0 to 1
- node_types: int32 [64, 128, 128], P('gy', 'gz'), may hold values from 0 to 3
Outputs:
- adjoint_prev: float32 [27, 64, 128, 128], P(None, 'gy', 'gz')
- sensitivity: float32 [64, 128, 128], P('gy', 'gz')
Inputs may be any that keep to these rules, and one draw needn't show every extreme that they name: `ckpt_pops`: every population is positive.
All inputs are finite; a program needn't handle non-finite values.
Results may differ from a plain program's by a relative error of at most 0.0003.
Values sent between devices are 32-bit elements; how exact they have to be, the bound alone decides.
A program may use at most 64 MiB of HBM per device.

v0:
```python
import jax
import jax.numpy as jnp
from jax import lax
from jax.sharding import PartitionSpec as P

RECOMP = 2


relax_rate = 1.0 / 0.6
brinkman = 4.0
inflow = 0.05


def with_halo(cells, sides, width):
    for axis, dim in sides:
        count = lax.axis_size(axis)
        head = lax.slice_in_dim(cells, 0, width, axis=dim)
        tail = lax.slice_in_dim(cells, cells.shape[dim] - width, cells.shape[dim], axis=dim)
        cells = jnp.concatenate(
            [
                lax.ppermute(tail, axis, [(i, (i + 1) % count) for i in range(count)]),
                cells,
                lax.ppermute(head, axis, [((i + 1) % count, i) for i in range(count)]),
            ],
            axis=dim,
        )
    return cells


def moment_line(values, shift):
    lower_v, middle, upper_v = (values[0], values[1], values[2])
    zeroth = lower_v + middle + upper_v
    linear = upper_v - lower_v - shift * zeroth
    square = upper_v + lower_v - 2.0 * shift * (upper_v - lower_v) + shift * shift * zeroth
    return jnp.stack([zeroth, linear, square])


def rebuild_line(moments, shift):
    zeroth, linear, square = (moments[0], moments[1], moments[2])
    lower_v = 0.5 * ((shift * shift - shift) * zeroth + (2.0 * shift - 1.0) * linear + square)
    middle = (1.0 - shift * shift) * zeroth - 2.0 * shift * linear - square
    upper_v = 0.5 * ((shift * shift + shift) * zeroth + (2.0 * shift + 1.0) * linear + square)
    return jnp.stack([lower_v, middle, upper_v])


def along_axis(values, axis_pos, func, shift):
    moved = jnp.moveaxis(values, axis_pos, 0)
    return jnp.moveaxis(func(moved, shift), 0, axis_pos)


def central(populations, speed_x, speed_y, speed_z):
    result = along_axis(populations, 0, moment_line, speed_x)
    result = along_axis(result, 1, moment_line, speed_y)
    return along_axis(result, 2, moment_line, speed_z)


def rebuild(moments, speed_x, speed_y, speed_z):
    result = along_axis(moments, 2, rebuild_line, speed_z)
    result = along_axis(result, 1, rebuild_line, speed_y)
    return along_axis(result, 0, rebuild_line, speed_x)


def gaussian_table(density, sxx, syy, szz, sxy, sxz, syz):
    nought = jnp.zeros_like(density)
    inverse = 1.0 / density
    entries = {
        (0, 0, 0): density,
        (2, 0, 0): sxx,
        (0, 2, 0): syy,
        (0, 0, 2): szz,
        (1, 1, 0): sxy,
        (1, 0, 1): sxz,
        (0, 1, 1): syz,
        (2, 2, 0): (sxx * syy + 2.0 * sxy * sxy) * inverse,
        (2, 0, 2): (sxx * szz + 2.0 * sxz * sxz) * inverse,
        (0, 2, 2): (syy * szz + 2.0 * syz * syz) * inverse,
        (2, 1, 1): (sxx * syz + 2.0 * sxy * sxz) * inverse,
        (1, 2, 1): (syy * sxz + 2.0 * sxy * syz) * inverse,
        (1, 1, 2): (szz * sxy + 2.0 * sxz * syz) * inverse,
        (2, 2, 2): (
            sxx * syy * szz
            + 2.0 * sxx * syz * syz
            + 2.0 * syy * sxz * sxz
            + 2.0 * szz * sxy * sxy
            + 8.0 * sxy * sxz * syz
        )
        * inverse
        * inverse,
    }
    planes = []
    for first in range(3):
        row_list = []
        for second in range(3):
            row_list.append(
                jnp.stack([entries.get((first, second, third), nought) for third in range(3)])
            )
        planes.append(jnp.stack(row_list))
    return jnp.stack(planes)


def collide(populations, design, node):
    density = jnp.sum(populations, axis=(0, 1, 2))
    speed_x = (
        jnp.sum(populations[2], axis=(0, 1)) - jnp.sum(populations[0], axis=(0, 1))
    ) / density
    speed_y = (
        jnp.sum(populations[:, 2], axis=(0, 1)) - jnp.sum(populations[:, 0], axis=(0, 1))
    ) / density
    speed_z = (
        jnp.sum(populations[:, :, 2], axis=(0, 1)) - jnp.sum(populations[:, :, 0], axis=(0, 1))
    ) / density
    moments = central(populations, speed_x, speed_y, speed_z)
    third_rho = density / 3.0
    sxx = moments[2, 0, 0] + relax_rate * (third_rho - moments[2, 0, 0])
    syy = moments[0, 2, 0] + relax_rate * (third_rho - moments[0, 2, 0])
    szz = moments[0, 0, 2] + relax_rate * (third_rho - moments[0, 0, 2])
    sxy = (1.0 - relax_rate) * moments[1, 1, 0]
    sxz = (1.0 - relax_rate) * moments[1, 0, 1]
    syz = (1.0 - relax_rate) * moments[0, 1, 1]
    keeping = 1.0 / (1.0 + brinkman * (1.0 - design))
    fluid = rebuild(
        gaussian_table(density, sxx, syy, szz, sxy, sxz, syz),
        speed_x * keeping,
        speed_y * keeping,
        speed_z * keeping,
    )
    unity = jnp.ones_like(density)
    nought = jnp.zeros_like(density)
    third = unity / 3.0
    resting = gaussian_table(unity, third, third, third, nought, nought, nought)
    outlet = rebuild(resting, speed_x, speed_y, speed_z)
    inlet = rebuild(resting, inflow * unity, nought, nought)
    bounce = populations[::-1, ::-1, ::-1]
    return jnp.where(
        node == 1, bounce, jnp.where(node == 2, inlet, jnp.where(node == 3, outlet, fluid))
    )


def shift_crop(padded, sign, offset, span_y, span_z):
    planes = []
    for vel_x in range(3):
        row_list = []
        for vel_y in range(3):
            column_list = []
            for vel_z in range(3):
                start_y = offset - sign * (vel_y - 1)
                start_z = offset - sign * (vel_z - 1)
                sliced = padded[
                    vel_x, vel_y, vel_z, start_y : start_y + span_y, start_z : start_z + span_z
                ]
                column_list.append(jnp.roll(sliced, sign * (vel_x - 1), axis=2))
            row_list.append(jnp.stack(column_list))
        planes.append(jnp.stack(row_list))
    return jnp.stack(planes)


def local(ckpt_pops, adjoint_pops, design, node_types):
    cell_shape = ckpt_pops.shape[1:]
    span_y = cell_shape[0]
    span_z = cell_shape[1]
    cell_data = jnp.stack([design, node_types.astype(jnp.float32)])
    stacked = jnp.concatenate([ckpt_pops, adjoint_pops, cell_data], axis=0)
    padded = with_halo(stacked, (("gy", 1), ("gz", 2)), RECOMP)
    primal = padded[:27].reshape((3, 3, 3) + padded.shape[1:])
    adjoint_wide = padded[27:54].reshape((3, 3, 3) + padded.shape[1:])
    design_wide = padded[54]
    node_wide = padded[55]
    for step in range(RECOMP):
        width_y = span_y + 2 * (RECOMP - step)
        width_z = span_z + 2 * (RECOMP - step)
        design_now = design_wide[step : step + width_y, step : step + width_z]
        node_now = node_wide[step : step + width_y, step : step + width_z]
        primal = shift_crop(collide(primal, design_now, node_now), 1, 1, width_y - 2, width_z - 2)
    pulled = shift_crop(adjoint_wide, -1, RECOMP, span_y, span_z)

    def local_collide(popul, shape_field):
        return collide(popul, shape_field, node_types)

    _, backward = jax.vjp(local_collide, primal, design)
    adjoint_prev, sensitivity = backward(pulled)
    return (adjoint_prev.reshape(ckpt_pops.shape), sensitivity)


def solution(mesh):
    return jax.shard_map(
        local,
        mesh=mesh,
        in_specs=(
            P(None, "gy", "gz", None),
            P(None, "gy", "gz", None),
            P("gy", "gz", None),
            P("gy", "gz", None),
        ),
        out_specs=(P(None, "gy", "gz", None), P("gy", "gz", None)),
        check_vma=False,
    )
```

profile of v0, /device:TPU:8, one launch (start us, length us, event | category | flops | bytes accessed | tf_op | source)
XLA Modules:
  0.0 74.4 jit_solution(5119096029516651927)
XLA Ops:
  0.6 0.7 convert_bitcast_fusion
  1.3 1.1 %pad_maximum_fusion.2 = f32[56,2,8,128]{3,2,1,0:T(8,128)S(1)} fusion(f32[1,2,8,128]{3,2,1,0:T(8,128)S(1)} %convert_bitcast_fusion, f32[1,2,8,128]{3,2,1,0:T(8,128)} %bitcast.2301, f32[27,2,8,128]{3,2,1,0:T(8,128)} %param.5, f32[27,2,8,128]{3,2,1,0:T(8,128)} %param.4), kind=kLoop, calls=%fused_computation.38 | loop fusion | flops 344064 | bytes 917504 | tf_op jit(solution)/shard_map/concatenate | solution.py:162
  2.5 6.9 %collective-permute-start.1 = (f32[56,2,8,128]{3,2,1,0:T(8,128)S(1)}, f32[56,2,8,128]{3,2,1,0:T(8,128)S(1)}, u32[]{:S(2)}, u32[]{:S(2)}) collective-permute-start(f32[56,2,8,128]{3,2,1,0:T(8,128)S(1)} %pad_maximum_fusion.2), channel_id=1, source_target_pairs={{16,0},{32,16},{48,32},{64,48},{80,64},{96,80},{112,96},{128,112},... | collective-permute-start | bytes 1376264 | tf_op jit(solution)/shard_map/ppermute | solution.py:23
  9.4 1.9 %collective-permute-start = (f32[56,2,8,128]{3,2,1,0:T(8,128)S(1)}, f32[56,2,8,128]{3,2,1,0:T(8,128)S(1)}, u32[]{:S(2)}, u32[]{:S(2)}) collective-permute-start(f32[56,2,8,128]{3,2,1,0:T(8,128)S(1)} %pad_maximum_fusion.2), channel_id=1, source_target_pairs={{0,16},{16,32},{32,48},{48,64},{64,80},{80,96},{96,112},{112,128},... | collective-permute-start | bytes 1376264 | tf_op jit(solution)/shard_map/ppermute | solution.py:21
  11.3 7.4 %collective-permute-done.1 = f32[56,2,8,128]{3,2,1,0:T(8,128)S(1)} collective-permute-done((f32[56,2,8,128]{3,2,1,0:T(8,128)S(1)}, f32[56,2,8,128]{3,2,1,0:T(8,128)S(1)}, u32[]{:S(2)}, u32[]{:S(2)}) %collective-permute-start.1) | collective-permute-done | bytes 458784 | tf_op jit(solution)/shard_map/ppermute | solution.py:23
  18.7 9.6 %collective-permute-done = f32[56,2,8,128]{3,2,1,0:T(8,128)S(1)} collective-permute-done((f32[56,2,8,128]{3,2,1,0:T(8,128)S(1)}, f32[56,2,8,128]{3,2,1,0:T(8,128)S(1)}, u32[]{:S(2)}, u32[]{:S(2)}) %collective-permute-start) | collective-permute-done | bytes 458784 | tf_op jit(solution)/shard_map/ppermute | solution.py:21
  28.3 1.5 %pad_maximum_fusion.13 = (f32[56,6,2,128]{3,2,1,0:T(2,128)S(1)}, f32[56,6,2,128]{3,2,1,0:T(2,128)S(1)}) fusion(f32[56,2,8,128]{3,2,1,0:T(8,128)S(1)} %collective-permute-done.1, f32[56,2,8,128]{3,2,1,0:T(8,128)S(1)} %collective-permute-done, f32[1,2,8,128]{3,2,1,0:T(8,128)S(1)} %convert_bitcast_fusion, f32[1,2,8,128]{3,2,1,0:T(8,128)} %bitcast.2302, ...), kind=kLoop, calls=%fused_computation.93 | loop fusion | flops 860160 | bytes 2064384 | tf_op jit(solution)/shard_map/slice | solution.py:18
  29.9 4.3 %collective-permute-start.2 = (f32[56,6,2,128]{3,2,1,0:T(2,128)S(1)}, f32[56,6,2,128]{3,2,1,0:T(2,128)S(1)}, u32[]{:S(2)}, u32[]{:S(2)}) collective-permute-start(f32[56,6,2,128]{3,2,1,0:T(2,128)S(1)} %get-tuple-element.178), channel_id=1, source_target_pairs={{0,1},{1,2},{2,3},{3,4},{4,5},{5,6},{6,7},{7,8},{8,9},{9,10},{10,1... | collective-permute-start | bytes 1032200 | tf_op jit(solution)/shard_map/ppermute | solution.py:21
  34.2 8.5 %collective-permute-start.3 = (f32[56,6,2,128]{3,2,1,0:T(2,128)S(1)}, f32[56,6,2,128]{3,2,1,0:T(2,128)S(1)}, u32[]{:S(2)}, u32[]{:S(2)}) collective-permute-start(f32[56,6,2,128]{3,2,1,0:T(2,128)S(1)} %get-tuple-element.179), channel_id=1, source_target_pairs={{1,0},{2,1},{3,2},{4,3},{5,4},{6,5},{7,6},{8,7},{9,8},{10,9},{11,1... | collective-permute-start | bytes 1032200 | tf_op jit(solution)/shard_map/ppermute | solution.py:23
  42.7 3.3 %collective-permute-done.2 = f32[56,6,2,128]{3,2,1,0:T(2,128)S(1)} collective-permute-done((f32[56,6,2,128]{3,2,1,0:T(2,128)S(1)}, f32[56,6,2,128]{3,2,1,0:T(2,128)S(1)}, u32[]{:S(2)}, u32[]{:S(2)}) %collective-permute-start.2) | collective-permute-done | bytes 344096 | tf_op jit(solution)/shard_map/ppermute | solution.py:21
  45.9 1.5 %collective-permute-done.3 = f32[56,6,2,128]{3,2,1,0:T(2,128)S(1)} collective-permute-done((f32[56,6,2,128]{3,2,1,0:T(2,128)S(1)}, f32[56,6,2,128]{3,2,1,0:T(2,128)S(1)}, u32[]{:S(2)}, u32[]{:S(2)}) %collective-permute-start.3) | collective-permute-done | bytes 344096 | tf_op jit(solution)/shard_map/ppermute | solution.py:23
  47.4 0.5 pad_maximum_fusion
  47.9 0.1 slice_reduce_fusion.12
  48.0 0.2 fusion.509
  48.8 0.1 maximum_bitcast_fusion.2
  48.9 0.1 multiply_subtract_fusion.1
  49.1 0.8 %copy-done.4 = f32[1,3,3,6,12,128]{5,4,3,0,2,1:T(8,128)S(1)} copy-done((f32[1,3,3,6,12,128]{5,4,3,0,2,1:T(8,128)S(1)}, f32[1,3,3,6,12,128]{5,4,3,0,2,1:T(8,128)}, u32[]{:S(2)}) %copy-start.4) | copy-done | bytes 331800
  49.9 0.1 copy-done.5
  50.0 0.1 copy-done.6
  50.2 0.2 bitcast_multiply_fusion.5
  50.4 0.1 maximum_bitcast_fusion
  50.5 0.3 bitcast_multiply_fusion.2
  51.1 0.1 maximum_bitcast_fusion.4
  52.0 0.1 fusion.10
  52.2 0.1 maximum_bitcast_fusion.6
  52.4 0.1 fusion.7
  52.6 0.1 maximum_bitcast_fusion.7
  52.7 0.2 add_multiply_fusion.3
  52.9 0.2 add_multiply_fusion.1
  53.1 1.1 %copy-done.2 = f32[3,3,3,6,12,128]{5,4,3,2,1,0:T(8,128)S(1)} copy-done((f32[3,3,3,6,12,128]{5,4,3,2,1,0:T(8,128)S(1)}, f32[3,3,3,6,12,128]{5,4,3,2,1,0:T(8,128)}, u32[]{:S(2)}) %copy-start.2) | copy-done | bytes 995352
  54.2 0.5 fusion.1
  58.4 0.3 multiply_subtract_fusion.20
  59.3 0.8 %copy-done.8 = f32[1,3,3,4,10,128]{5,4,3,0,2,1:T(8,128)S(1)} copy-done((f32[1,3,3,4,10,128]{5,4,3,0,2,1:T(8,128)S(1)}, f32[1,3,3,4,10,128]{5,4,3,0,2,1:T(8,128)}, u32[]{:S(2)}) %copy-start.8) | copy-done | bytes 184344
  60.2 0.1 bitcast_multiply_fusion.13
  60.4 0.2 bitcast_multiply_fusion.9
  61.0 0.3 fusion.234
  61.7 0.2 bitcast_multiply_fusion.11
  62.0 0.2 bitcast_multiply_fusion.7
  62.2 0.2 add_multiply_fusion.7
  62.4 0.2 add_multiply_fusion.5
  62.6 1.0 %copy-done.3 = f32[3,3,3,4,10,128]{5,4,3,2,1,0:T(8,128)S(1)} copy-done((f32[3,3,3,4,10,128]{5,4,3,2,1,0:T(8,128)S(1)}, f32[3,3,3,4,10,128]{5,4,3,2,1,0:T(8,128)}, u32[]{:S(2)}) %copy-start.3) | copy-done | bytes 552984
  63.6 0.4 fusion.3
  68.3 0.1 broadcast_multiply_fusion.16
  70.2 0.2 fusion.374
  70.9 0.1 fusion.437
  71.8 0.6 copy-done.11
  72.8 0.6 multiply_negate_fusion
  73.6 0.8 %add_add_fusion.1 = f32[3,3,3,2,8,128]{5,4,3,2,1,0:T(8,128)} fusion(f32[1,3,3,2,8,128]{5,4,3,2,1,0:T(8,128)S(1)} %broadcast_in_dim.62, f32[1,3,3,2,8,128]{5,4,3,2,1,0:T(8,128)S(1)} %broadcast_in_dim.61, f32[3,1,3,2,8,128]{5,4,3,2,1,0:T(8,128)S(1)} %broadcast_in_dim.60, f32[3,1,3,2,8,128]{5,4,3,2,1,0:T(8,128)S(1)} %broadcast_in_dim.59, ...), kind=kLoop, calls=%fused_computation.171 | loop fusion | flops 552960 | bytes 1114112 | tf_op jit(solution)/shard_map/transpose(jvp())/add_any | solution.py:102
  (348 shorter events, 13.9 us)
Async XLA Ops:
  1.3 41.3 %copy-start.16 = (s32[2,8,128]{2,1,0:T(8,128)S(1)}, s32[2,8,128]{2,1,0:T(8,128)}, u32[]{:S(2)}) copy-start(s32[2,8,128]{2,1,0:T(8,128)} %param.7) | copy-start | bytes 24580
  1.3 46.0 %copy-start = (f32[27,2,8,128]{3,2,1,0:T(8,128)S(1)}, f32[27,2,8,128]{3,2,1,0:T(8,128)}, u32[]{:S(2)}) copy-start(f32[27,2,8,128]{3,2,1,0:T(8,128)} %param.5) | copy-start | bytes 663556
  1.3 46.0 %copy-start.1 = (f32[27,2,8,128]{3,2,1,0:T(8,128)S(1)}, f32[27,2,8,128]{3,2,1,0:T(8,128)}, u32[]{:S(2)}) copy-start(f32[27,2,8,128]{3,2,1,0:T(8,128)} %param.4) | copy-start | bytes 663556
  1.3 46.0 %copy-start.7 = (f32[2,8,128]{2,1,0:T(8,128)S(1)}, f32[2,8,128]{2,1,0:T(8,128)}, u32[]{:S(2)}) copy-start(f32[2,8,128]{2,1,0:T(8,128)} %param.6) | copy-start | bytes 24580
  2.5 16.2 %collective-permute-start.1 = (f32[56,2,8,128]{3,2,1,0:T(8,128)S(1)}, f32[56,2,8,128]{3,2,1,0:T(8,128)S(1)}, u32[]{:S(2)}, u32[]{:S(2)}) collective-permute-start(f32[56,2,8,128]{3,2,1,0:T(8,128)S(1)} %pad_maximum_fusion.2), channel_id=1, source_target_pairs={{16,0},{32,16},{48,32},{64,48},{80,64},{96,80},{112,96},{128,112},... | collective-permute-start | bytes 1376264 | tf_op jit(solution)/shard_map/ppermute | solution.py:23
  9.4 18.9 %collective-permute-start = (f32[56,2,8,128]{3,2,1,0:T(8,128)S(1)}, f32[56,2,8,128]{3,2,1,0:T(8,128)S(1)}, u32[]{:S(2)}, u32[]{:S(2)}) collective-permute-start(f32[56,2,8,128]{3,2,1,0:T(8,128)S(1)} %pad_maximum_fusion.2), channel_id=1, source_target_pairs={{0,16},{16,32},{32,48},{48,64},{64,80},{80,96},{96,112},{112,128},... | collective-permute-start | bytes 1376264 | tf_op jit(solution)/shard_map/ppermute | solution.py:21
  29.9 16.0 %collective-permute-start.2 = (f32[56,6,2,128]{3,2,1,0:T(2,128)S(1)}, f32[56,6,2,128]{3,2,1,0:T(2,128)S(1)}, u32[]{:S(2)}, u32[]{:S(2)}) collective-permute-start(f32[56,6,2,128]{3,2,1,0:T(2,128)S(1)} %get-tuple-element.178), channel_id=1, source_target_pairs={{0,1},{1,2},{2,3},{3,4},{4,5},{5,6},{6,7},{7,8},{8,9},{9,10},{10,1... | collective-permute-start | bytes 1032200 | tf_op jit(solution)/shard_map/ppermute | solution.py:21
  34.2 13.2 %collective-permute-start.3 = (f32[56,6,2,128]{3,2,1,0:T(2,128)S(1)}, f32[56,6,2,128]{3,2,1,0:T(2,128)S(1)}, u32[]{:S(2)}, u32[]{:S(2)}) collective-permute-start(f32[56,6,2,128]{3,2,1,0:T(2,128)S(1)} %get-tuple-element.179), channel_id=1, source_target_pairs={{1,0},{2,1},{3,2},{4,3},{5,4},{6,5},{7,6},{8,7},{9,8},{10,9},{11,1... | collective-permute-start | bytes 1032200 | tf_op jit(solution)/shard_map/ppermute | solution.py:23
  48.9 1.0 %copy-start.4 = (f32[1,3,3,6,12,128]{5,4,3,0,2,1:T(8,128)S(1)}, f32[1,3,3,6,12,128]{5,4,3,0,2,1:T(8,128)}, u32[]{:S(2)}) copy-start(f32[1,3,3,6,12,128]{5,4,3,0,2,1:T(8,128)} %constant.346.clone.1) | copy-start | bytes 995332
  48.9 1.1 %copy-start.5 = (f32[1,3,3,6,12,128]{5,4,3,0,2,1:T(8,128)S(1)}, f32[1,3,3,6,12,128]{5,4,3,0,2,1:T(8,128)}, u32[]{:S(2)}) copy-start(f32[1,3,3,6,12,128]{5,4,3,0,2,1:T(8,128)} %constant.344.clone.1) | copy-start | bytes 995332
  48.9 1.3 %copy-start.6 = (f32[1,3,3,6,12,128]{5,4,3,0,2,1:T(8,128)S(1)}, f32[1,3,3,6,12,128]{5,4,3,0,2,1:T(8,128)}, u32[]{:S(2)}) copy-start(f32[1,3,3,6,12,128]{5,4,3,0,2,1:T(8,128)} %constant.342.clone.1) | copy-start | bytes 995332
  52.9 1.3 %copy-start.2 = (f32[3,3,3,6,12,128]{5,4,3,2,1,0:T(8,128)S(1)}, f32[3,3,3,6,12,128]{5,4,3,2,1,0:T(8,128)}, u32[]{:S(2)}) copy-start(f32[3,3,3,6,12,128]{5,4,3,2,1,0:T(8,128)} %constant.340.clone.1) | copy-start | bytes 2985988
  59.1 1.0 %copy-start.8 = (f32[1,3,3,4,10,128]{5,4,3,0,2,1:T(8,128)S(1)}, f32[1,3,3,4,10,128]{5,4,3,0,2,1:T(8,128)}, u32[]{:S(2)}) copy-start(f32[1,3,3,4,10,128]{5,4,3,0,2,1:T(8,128)} %constant.356.clone.1) | copy-start | bytes 552964
  59.1 1.0 %copy-start.9 = (f32[1,3,3,4,10,128]{5,4,3,0,2,1:T(8,128)S(1)}, f32[1,3,3,4,10,128]{5,4,3,0,2,1:T(8,128)}, u32[]{:S(2)}) copy-start(f32[1,3,3,4,10,128]{5,4,3,0,2,1:T(8,128)} %constant.355.clone.1) | copy-start | bytes 552964
  59.1 1.1 %copy-start.10 = (f32[1,3,3,4,10,128]{5,4,3,0,2,1:T(8,128)S(1)}, f32[1,3,3,4,10,128]{5,4,3,0,2,1:T(8,128)}, u32[]{:S(2)}) copy-start(f32[1,3,3,4,10,128]{5,4,3,0,2,1:T(8,128)} %constant.354.clone.1) | copy-start | bytes 552964
  62.4 1.2 %copy-start.3 = (f32[3,3,3,4,10,128]{5,4,3,2,1,0:T(8,128)S(1)}, f32[3,3,3,4,10,128]{5,4,3,2,1,0:T(8,128)}, u32[]{:S(2)}) copy-start(f32[3,3,3,4,10,128]{5,4,3,2,1,0:T(8,128)} %constant.353.clone.1) | copy-start | bytes 1658884
  71.5 0.9 %copy-start.11 = (f32[1,3,3,2,8,128]{5,4,3,2,1,0:T(8,128)S(1)}, f32[1,3,3,2,8,128]{5,4,3,2,1,0:T(8,128)}, u32[]{:S(2)}) copy-start(f32[1,3,3,2,8,128]{5,4,3,2,1,0:T(8,128)} %constant.446) | copy-start | bytes 221188
  71.5 0.9 %copy-start.12 = (f32[1,3,3,2,8,128]{5,4,3,2,1,0:T(8,128)S(1)}, f32[1,3,3,2,8,128]{5,4,3,2,1,0:T(8,128)}, u32[]{:S(2)}) copy-start(f32[1,3,3,2,8,128]{5,4,3,2,1,0:T(8,128)} %constant.361.clone.1) | copy-start | bytes 221188
  71.6 0.9 %copy-start.13 = (f32[1,3,3,2,8,128]{5,4,3,0,2,1:T(8,128)S(1)}, f32[1,3,3,2,8,128]{5,4,3,0,2,1:T(8,128)}, u32[]{:S(2)}) copy-start(f32[1,3,3,2,8,128]{5,4,3,0,2,1:T(8,128)} %constant.447) | copy-start | bytes 221188
  71.6 0.9 %copy-start.14 = (f32[1,3,3,2,8,128]{5,4,3,0,2,1:T(8,128)S(1)}, f32[1,3,3,2,8,128]{5,4,3,0,2,1:T(8,128)}, u32[]{:S(2)}) copy-start(f32[1,3,3,2,8,128]{5,4,3,0,2,1:T(8,128)} %constant.362.clone.1) | copy-start | bytes 221188
  71.6 1.0 %copy-start.15 = (f32[1,3,3,2,8,128]{5,4,3,0,2,1:T(8,128)S(1)}, f32[1,3,3,2,8,128]{5,4,3,0,2,1:T(8,128)}, u32[]{:S(2)}) copy-start(f32[1,3,3,2,8,128]{5,4,3,0,2,1:T(8,128)} %constant.360.clone.1) | copy-start | bytes 221188
where the time goes:
time: 74.9 us; the launch traced here: 74.4 us
  waiting for transfers between devices  21.7 us (29%)
  starting transfers between devices  21.6 us (29%)
  other arithmetic  19.5 us (26%)
  local copies, waits for them, and re-layouts  9.21 us (12%)
  between operations  2.37 us (3%)
    ppermute x2, starting transfers between devices, with_halo(): lax.ppermute(head, axis, [((i + 1) % count, i) for i in range(count)])  15.4 us
    ppermute x2, waiting for transfers between devices, with_halo(): lax.ppermute(tail, axis, [(i, (i + 1) % count) for i in range(count)])  12.9 us
    ppermute x2, waiting for transfers between devices, with_halo(): lax.ppermute(head, axis, [((i + 1) % count, i) for i in range(count)])  8.83 us
    ppermute x2, starting transfers between devices, with_halo(): lax.ppermute(tail, axis, [(i, (i + 1) % count) for i in range(count)])  6.2 us
    unnamed x34, local copies, waits for them, and re-layouts  4.88 us
    another operation x48, other arithmetic, shift_crop(): row_list.append(jnp.stack(column_list))  3.69 us
    concatenate x72, local copies, waits for them, and re-layouts, shift_crop(): column_list.append(jnp.roll(sliced, sign * (vel_x - 1), axis=2))  2.81 us
    mul x15, other arithmetic, rebuild_line(): 0.5 * ((shift * shift - shift) * zeroth + (2.0 * shift - 1.0) * linear +...  2.3 us
  transfers between devices with their start and end apart: 4, of which 4 were waited for; matrix products, arithmetic and copies ran while one was open for 0% of the time, Pallas kernels for 0%

commit v1 on v0

v1 whole, which is shorter than its diff:
```python
import jax
import jax.numpy as jnp
from jax import lax
from jax.experimental import pallas as pl
from jax.experimental.pallas import tpu as pltpu
from jax.sharding import PartitionSpec as P

relax_rate = 1.0 / 0.6
brinkman = 4.0
inflow = 0.05

MESH = pl.DeviceIdType.MESH
SIDES = [(1, 0), (-1, 0), (0, 1), (0, -1), (1, 1), (1, -1), (-1, 1), (-1, -1)]
KEPT = [(1, 0), (1, 1), (2, 0), (0, 1)]


def full(like, value):
    return jnp.full(like.shape, value, like.dtype)


def rebuild_line(zeroth, linear, square, shift):
    if zeroth is None:
        twice = shift * (linear + linear)
        if square is not None:
            twice = twice + square
        return 0.5 * (twice - linear), -twice, 0.5 * (twice + linear)
    odd = shift * zeroth
    if linear is None:
        even = shift * odd
    else:
        odd = odd + linear
        even = shift * (odd + linear)
    if square is not None:
        even = even + square
    return 0.5 * (even - odd), zeroth - even, 0.5 * (even + odd)


def collide(f, design, node):
    z0, z1, z2 = [], [], []
    for ab in range(9):
        lower, middle, upper = f[3 * ab : 3 * ab + 3]
        ends = upper + lower
        z0.append(ends + middle)
        z1.append(upper - lower)
        z2.append(ends)
    y00, y10, y20, y01, y11, y02 = [], [], [], [], [], []
    for a in range(3):
        ends = z0[3 * a + 2] + z0[3 * a]
        y00.append(ends + z0[3 * a + 1])
        y10.append(z0[3 * a + 2] - z0[3 * a])
        y20.append(ends)
        y01.append(z1[3 * a] + z1[3 * a + 1] + z1[3 * a + 2])
        y11.append(z1[3 * a + 2] - z1[3 * a])
        y02.append(z2[3 * a] + z2[3 * a + 1] + z2[3 * a + 2])
    m200 = y00[2] + y00[0]
    rho = m200 + y00[1]
    jx = y00[2] - y00[0]
    jy = y10[0] + y10[1] + y10[2]
    m110 = y10[2] - y10[0]
    m020 = y20[0] + y20[1] + y20[2]
    jz = y01[0] + y01[1] + y01[2]
    m101 = y01[2] - y01[0]
    m011 = y11[0] + y11[1] + y11[2]
    m002 = y02[0] + y02[1] + y02[2]

    inverse = 1.0 / rho
    ux, uy, uz = jx * inverse, jy * inverse, jz * inverse
    keep_rate = 1.0 - relax_rate
    base = (relax_rate / 3.0) * rho
    sxx = keep_rate * (m200 - jx * ux) + base
    syy = keep_rate * (m020 - jy * uy) + base
    szz = keep_rate * (m002 - jz * uz) + base
    sxy = keep_rate * (m110 - jx * uy)
    sxz = keep_rate * (m101 - jx * uz)
    syz = keep_rate * (m011 - jy * uz)

    fluid = node == 0
    one, nought, third = full(rho, 1.0), full(rho, 0.0), full(rho, 1.0 / 3.0)
    rho = lax.select(fluid, rho, one)
    inverse = lax.select(fluid, inverse, one)
    sxx = lax.select(fluid, sxx, third)
    syy = lax.select(fluid, syy, third)
    szz = lax.select(fluid, szz, third)
    sxy = lax.select(fluid, sxy, nought)
    sxz = lax.select(fluid, sxz, nought)
    syz = lax.select(fluid, syz, nought)
    keeping = 1.0 / (1.0 + brinkman * (1.0 - design))
    factor = lax.select(fluid, keeping, lax.select(node == 3, one, nought))
    vx = ux * factor + lax.select(node == 2, full(rho, inflow), nought)
    vy = uy * factor
    vz = uz * factor

    dxy, dxz, dyz = sxy + sxy, sxz + sxz, syz + syz
    fxy, fxz, fyz = dxy * sxy, dxz * sxz, dyz * syz
    g220 = (sxx * syy + fxy) * inverse
    g202 = (sxx * szz + fxz) * inverse
    g022 = (syy * szz + fyz) * inverse
    g211 = (sxx * syz + dxy * sxz) * inverse
    g121 = (syy * sxz + dxy * syz) * inverse
    g112 = (szz * sxy + dxz * syz) * inverse
    g222 = (
        (sxx * (syy * szz + fyz) + syy * fxz + szz * fxy + 2.0 * (dxy * dxz) * syz)
        * inverse
        * inverse
    )
    lines = {
        (0, 0): (rho, None, szz),
        (2, 0): (sxx, None, g202),
        (0, 2): (syy, None, g022),
        (2, 2): (g220, None, g222),
        (1, 1): (sxy, None, g112),
        (1, 0): (None, sxz, None),
        (0, 1): (None, syz, None),
        (2, 1): (None, g211, None),
        (1, 2): (None, g121, None),
    }
    along_z = {key: rebuild_line(*value, vz) for key, value in lines.items()}
    result = [None] * 27
    along_y = {
        (p, c): rebuild_line(along_z[p, 0][c], along_z[p, 1][c], along_z[p, 2][c], vy)
        for p in range(3)
        for c in range(3)
    }
    for b in range(3):
        for c in range(3):
            line = rebuild_line(along_y[0, c][b], along_y[1, c][b], along_y[2, c][b], vx)
            for a in range(3):
                result[9 * a + 3 * b + c] = line[a]
    solid = node == 1
    return [lax.select(solid, f[26 - i], result[i]) for i in range(27)]


def edge(step, last):
    return last if step > 0 else 0


def pack(tile, rows_z, rows_d):
    for way, step in enumerate((1, -1)):
        z, c = edge(step, 7), 1 + step
        for k, (b, y) in enumerate(KEPT):
            for a in range(3):
                rows_z[way, 3 * k + a : 3 * k + a + 1, :] = tile(a, b, c, y)[z : z + 1, :]
        for turn, step_y in enumerate((1, -1)):
            corner = 2 * turn + way
            for a in range(3):
                rows_d[corner, a : a + 1, :] = tile(a, 1 + step_y, c, edge(step_y, 1))[z : z + 1, :]


def arrive(tile, got_y, got_z, got_d, a, b, c, y, row):
    source = y - (b - 1)
    inside = 0 <= source < 2
    turn = 0 if b == 2 else 1
    value = tile(a, b, c, source) if inside else got_y[turn, a, c]
    if c != 1:
        way = 0 if c == 2 else 1
        if inside:
            k = 3 * KEPT.index((b, source)) + a
            line = got_z[way, k : k + 1, :]
        else:
            line = got_d[2 * turn + way, a : a + 1, :]
        value = pltpu.roll(value, 1 if c == 2 else 7, 0)
        value = jnp.where(row == (0 if c == 2 else 7), line, value)
    if a != 1:
        value = pltpu.roll(value, 1 if a == 2 else 127, 1)
    return value


def kernel(
    counts,
    ckpt,
    adjoint,
    design,
    node,
    previous,
    sensitivity,
    post,
    primal,
    pulled,
    got_y,
    put_z,
    got_z,
    put_d,
    got_d,
    send_sem,
    recv_sem,
):
    gy, gz = lax.axis_index("gy"), lax.axis_index("gz")
    near = [
        (lax.rem(gy + dy + counts[0], counts[0]), lax.rem(gz + dz + counts[1], counts[1]))
        for dy, dz in SIDES
    ]
    barrier = pltpu.get_barrier_semaphore()
    for who in near:
        pl.semaphore_signal(barrier, inc=1, device_id=who, device_id_type=MESH)

    def sends(turn, flat_y):
        sources = [
            (flat_y[0], got_y.at[turn, 0]),
            (flat_y[1], got_y.at[turn, 1]),
        ]
        sources += [(put_z.at[turn, way], got_z.at[turn, way]) for way in range(2)]
        sources += [(put_d.at[turn, way], got_d.at[turn, way]) for way in range(4)]
        copies = [
            pltpu.make_async_remote_copy(
                src_ref=src,
                dst_ref=dst,
                send_sem=send_sem.at[turn, i],
                recv_sem=recv_sem.at[turn, i],
                device_id=near[i],
                device_id_type=MESH,
            )
            for i, (src, dst) in enumerate(sources)
        ]
        for copy in reversed(copies):
            copy.start()
        return copies

    row = lax.broadcasted_iota(jnp.int32, (8, 128), 0)

    def collide_rows(load, turn):
        def body(y, carry):
            f = [load(i, y) for i in range(27)]
            h = collide(f, design[y], node[y])
            for i in range(27):
                post[turn, i // 3 % 3, y, i // 9, i % 3] = h[i]
            return carry

        lax.fori_loop(0, 2, body, 0)

    def post_tile(turn):
        return lambda a, b, c, y: post[turn, b, y, a, c]

    def gather(tile, turn, into, flip):
        for y in range(2):
            for i in range(27):
                a, b, c = i // 9, i // 3 % 3, i % 3
                value = arrive(
                    tile, got_y.at[turn], got_z.at[turn], got_d.at[turn], a, b, c, y, row
                )
                into[26 - i if flip else i, y] = value

    def adjoint_tile(a, b, c, y):
        return adjoint[2 - a, 2 - b, 2 - c, y]

    collide_rows(lambda i, y: ckpt[i // 9, i // 3 % 3, i % 3, y], 0)
    pack(post_tile(0), put_z.at[0], put_d.at[0])
    pl.semaphore_wait(barrier, len(near))
    first = sends(0, [post.at[0, 2, 1], post.at[0, 0, 0]])
    pack(adjoint_tile, put_z.at[2], put_d.at[2])
    third = sends(2, [adjoint.at[:, 0, :, 1], adjoint.at[:, 2, :, 0]])

    for copy in first:
        copy.wait_recv()
    gather(post_tile(0), 0, primal, False)

    collide_rows(lambda i, y: primal[i, y], 1)
    pack(post_tile(1), put_z.at[1], put_d.at[1])
    second = sends(1, [post.at[1, 2, 1], post.at[1, 0, 0]])

    for copy in third:
        copy.wait_recv()
    gather_adjoint(adjoint_tile, got_y.at[2], got_z.at[2], got_d.at[2], pulled, row)

    for copy in second:
        copy.wait_recv()
    gather(post_tile(1), 1, primal, False)

    def backward(y, carry):
        f = [primal[i, y] for i in range(27)]
        kind = node[y]
        _, pull = jax.vjp(lambda pops, field: collide(pops, field, kind), f, design[y])
        grads, slope = pull([pulled[i, y] for i in range(27)])
        for i in range(27):
            previous[i // 9, i // 3 % 3, i % 3, y] = grads[i]
        sensitivity[y] = slope
        return carry

    lax.fori_loop(0, 2, backward, 0)
    for copy in first + third + second:
        copy.wait_send()


class Reversed:
    def __init__(self, ref):
        self.ref = ref

    def __getitem__(self, key):
        turn, a, c = key
        return self.ref[turn, 2 - a, 2 - c]


def gather_adjoint(tile, got_y, got_z, got_d, into, row):
    for y in range(2):
        for i in range(27):
            a, b, c = i // 9, i // 3 % 3, i % 3
            value = arrive(tile, Reversed(got_y), got_z, got_d, a, b, c, y, row)
            into[26 - i, y] = value


def solution(mesh):
    counts = (mesh.shape["gy"], mesh.shape["gz"])

    def local(ckpt_pops, adjoint_pops, design, node_types):
        f32 = jnp.float32
        cells = ckpt_pops.shape[1:]
        whole = pl.BlockSpec(memory_space=pltpu.VMEM)
        previous, sensitivity = pl.pallas_call(
            lambda *refs: kernel(counts, *refs),
            out_shape=(
                jax.ShapeDtypeStruct((3, 3, 3) + cells, f32),
                jax.ShapeDtypeStruct(cells, f32),
            ),
            in_specs=[whole] * 4,
            out_specs=(whole, whole),
            scratch_shapes=[
                pltpu.VMEM((2, 3, 2, 3, 3, 8, 128), f32),
                pltpu.VMEM((27, 2, 8, 128), f32),
                pltpu.VMEM((27, 2, 8, 128), f32),
                pltpu.VMEM((3, 2, 3, 3, 8, 128), f32),
                pltpu.VMEM((3, 2, 16, 128), f32),
                pltpu.VMEM((3, 2, 16, 128), f32),
                pltpu.VMEM((3, 4, 8, 128), f32),
                pltpu.VMEM((3, 4, 8, 128), f32),
                pltpu.SemaphoreType.DMA((3, 8)),
                pltpu.SemaphoreType.DMA((3, 8)),
            ],
            compiler_params=pltpu.CompilerParams(collective_id=0, has_side_effects=True),
            name="adjoint_step",
        )(
            ckpt_pops.reshape((3, 3, 3) + cells),
            adjoint_pops.reshape((3, 3, 3) + cells),
            design,
            node_types,
        )
        return previous.reshape(ckpt_pops.shape), sensitivity

    return jax.shard_map(
        local,
        mesh=mesh,
        in_specs=(
            P(None, "gy", "gz", None),
            P(None, "gy", "gz", None),
            P("gy", "gz", None),
            P("gy", "gz", None),
        ),
        out_specs=(P(None, "gy", "gz", None), P("gy", "gz", None)),
        check_vma=False,
    )
```

time: 74.9 us -> 32.6 us (0.44)
  Pallas kernels: 0 us -> 29.6 us
  waiting for transfers between devices: 21.7 us -> 0 us
  starting transfers between devices: 21.6 us -> 0 us
  other arithmetic: 19.5 us -> 0 us
  local copies, waits for them, and re-layouts: 9.21 us -> 2.24 us
  between operations: 2.37 us -> 0.65 us
    pallas_call x0 -> x1, Pallas kernels: none -> 29.6 us  [local(): pl.pallas_call(lambda *refs: kernel(counts, *refs), out_shape=(jax.ShapeD...]
    ppermute x4 -> x0, waiting for transfers between devices: 21.7 us -> none  [the longest x2 12.9 us: with_halo(): lax.ppermute(tail, axis, [(i, (i + 1) % count) for i in range(count)])]
    ppermute x4 -> x0, starting transfers between devices: 21.6 us -> none  [the longest x2 15.4 us: with_halo(): lax.ppermute(head, axis, [((i + 1) % count, i) for i in range(count)])]
    another operation x107 -> x0, other arithmetic: 5.82 us -> none  [the longest x48 3.69 us: shift_crop(): row_list.append(jnp.stack(column_list))]
    mul x34 -> x0, other arithmetic: 3.48 us -> none  [the longest x15 2.3 us: rebuild_line(): 0.5 * ((shift * shift - shift) * zeroth + (2.0 * shift - 1.0) * linear +...]
    concatenate x72 -> x0, local copies, waits for them, and re-layouts: 2.81 us -> none  [shift_crop(): column_list.append(jnp.roll(sliced, sign * (vel_x - 1), axis=2))]
    unnamed x34 -> x4, local copies, waits for them, and re-layouts: 4.88 us -> 2.24 us
    slice x2 -> x0, other arithmetic: 1.73 us -> none  [the longest x1 1.54 us: with_halo(): lax.slice_in_dim(cells, cells.shape[dim] - width, cells.shape[dim], axis=...]
  transfers between devices with their start and end apart: 4 -> 0, of which waited for: 4 -> 0; matrix products, arithmetic and copies ran while one was open for 0% -> 0% of each run, Pallas kernels for 0% -> 0%
where the time goes in v1:
time: 32.6 us; the launch traced here: 32.4 us
  Pallas kernels  29.6 us (91%)
  local copies, waits for them, and re-layouts  2.24 us (7%)
  between operations  0.65 us (2%)
    pallas_call x1, Pallas kernels, local(): pl.pallas_call(lambda *refs: kernel(counts, *refs), out_shape=(jax.ShapeD...  29.6 us
    unnamed x4, local copies, waits for them, and re-layouts  2.24 us

profile of v1, /device:TPU:8, one launch (start us, length us, event | category | flops | bytes accessed | tf_op | source)
XLA Modules:
  0.0 32.4 jit_solution(10540626153175109332)
XLA Ops:
  0.6 29.6 %adjoint_step.1 = (f32[3,3,3,2,8,128]{5,4,3,2,1,0:T(8,128)}, f32[2,8,128]{2,1,0:T(8,128)}) custom-call(f32[3,3,3,2,8,128]{5,4,3,2,1,0:T(8,128)} %bitcast.3, f32[3,3,3,2,8,128]{5,4,3,2,1,0:T(8,128)} %bitcast.4, f32[2,8,128]{2,1,0:T(8,128)} %refs_2_.1, s32[2,8,128]{2,1,0:T(8,128)} %refs_3_.1), custom_call_target="tpu_custom_call" | custom-call | tf_op jit(solution)/shard_map/adjoint_step/pallas_call | solution.py:307
  30.2 0.0 copy-start
  30.2 1.6 %copy.8 = f32[27,2,8,128]{3,2,1,0:T(8,128)} copy(f32[27,2,8,128]{3,2,1,0:T(8,128)} %bitcast.5) | data formatting | bytes 442368
  31.8 0.0 copy-done
  31.8 0.6 %copy.9 = f32[2,8,128]{2,1,0:T(8,128)} copy(f32[2,8,128]{2,1,0:T(8,128)S(1)} %copy-done) | data formatting | bytes 16384
Async XLA Ops:
  30.2 1.7 %copy-start = (f32[2,8,128]{2,1,0:T(8,128)S(1)}, f32[2,8,128]{2,1,0:T(8,128)}, u32[]{:S(2)}) copy-start(f32[2,8,128]{2,1,0:T(8,128)} %get-tuple-element.9) | copy-start | bytes 24580

commit v2 on v1

--- a/solution.py
+++ b/solution.py
@@ -11,7 +11,6 @@
 
 MESH = pl.DeviceIdType.MESH
 SIDES = [(1, 0), (-1, 0), (0, 1), (0, -1), (1, 1), (1, -1), (-1, 1), (-1, -1)]
-KEPT = [(1, 0), (1, 1), (2, 0), (0, 1)]
 
 
 def full(like, value):
@@ -134,30 +133,54 @@
     return last if step > 0 else 0
 
 
-def pack(tile, rows_z, rows_d):
-    for way, step in enumerate((1, -1)):
-        z, c = edge(step, 7), 1 + step
+GROUPS = {1: [(1, 1), (2, 0), (2, 1)], -1: [(0, 0), (0, 1), (1, 0)]}
+CELL_ROW, BACK_ROW = 54, 58
+KEPT = [(1, 0), (1, 1), (2, 0), (0, 1)]
+TURNS = (1, -1)
+
+
+def moving(step, kind):
+    near, far = (7, 6) if step > 0 else (0, 1)
+    return [(far, 1 + step), (near, 1), (near, 1 + step)][kind]
+
+
+def pack(tile, back, design, node, rows_z, rows_d):
+    for way, step in enumerate(TURNS):
+        near = edge(step, 7)
+        for kind in range(3):
+            z, c = moving(step, kind)
+            for y in range(2):
+                for b in range(3):
+                    for a in range(3):
+                        k = 18 * kind + 9 * y + 3 * b + a
+                        rows_z[way, k : k + 1, :] = tile(a, b, c, y)[z : z + 1, :]
+        for y in range(2):
+            k = CELL_ROW + 2 * y
+            rows_z[way, k : k + 1, :] = design[y, near : near + 1, :]
+            rows_z[way, k + 1 : k + 2, :] = node[y, near : near + 1, :].astype(jnp.float32)
         for k, (b, y) in enumerate(KEPT):
             for a in range(3):
-                rows_z[way, 3 * k + a : 3 * k + a + 1, :] = tile(a, b, c, y)[z : z + 1, :]
-        for turn, step_y in enumerate((1, -1)):
+                at = BACK_ROW + 3 * k + a
+                rows_z[way, at : at + 1, :] = back(a, b, 1 + step, y)[near : near + 1, :]
+        for turn, step_y in enumerate(TURNS):
             corner = 2 * turn + way
+            for kind in range(3):
+                z, c = moving(step, kind)
+                for j, (b, y) in enumerate(GROUPS[step_y]):
+                    for a in range(3):
+                        k = 9 * kind + 3 * j + a
+                        rows_d[corner, k : k + 1, :] = tile(a, b, c, y)[z : z + 1, :]
+            y = edge(step_y, 1)
+            rows_d[corner, 27:28, :] = design[y, near : near + 1, :]
+            rows_d[corner, 28:29, :] = node[y, near : near + 1, :].astype(jnp.float32)
             for a in range(3):
-                rows_d[corner, a : a + 1, :] = tile(a, 1 + step_y, c, edge(step_y, 1))[z : z + 1, :]
-
-
-def arrive(tile, got_y, got_z, got_d, a, b, c, y, row):
-    source = y - (b - 1)
-    inside = 0 <= source < 2
-    turn = 0 if b == 2 else 1
-    value = tile(a, b, c, source) if inside else got_y[turn, a, c]
+                rows_d[corner, 29 + a : 30 + a, :] = back(a, 1 + step_y, 1 + step, y)[
+                    near : near + 1, :
+                ]
+
+
+def shifted(value, a, c, line, row):
     if c != 1:
-        way = 0 if c == 2 else 1
-        if inside:
-            k = 3 * KEPT.index((b, source)) + a
-            line = got_z[way, k : k + 1, :]
-        else:
-            line = got_d[2 * turn + way, a : a + 1, :]
         value = pltpu.roll(value, 1 if c == 2 else 7, 0)
         value = jnp.where(row == (0 if c == 2 else 7), line, value)
     if a != 1:
@@ -175,8 +198,13 @@
     sensitivity,
     post,
     primal,
+    wide_design,
+    wide_node,
+    ring_node,
+    second,
     pulled,
     got_y,
+    got_back,
     put_z,
     got_z,
     put_d,
@@ -193,77 +221,141 @@
     for who in near:
         pl.semaphore_signal(barrier, inc=1, device_id=who, device_id_type=MESH)
 
-    def sends(turn, flat_y):
-        sources = [
-            (flat_y[0], got_y.at[turn, 0]),
-            (flat_y[1], got_y.at[turn, 1]),
+    row = lax.broadcasted_iota(jnp.int32, (8, 128), 0)
+
+    def collide_first(y, carry):
+        f = [ckpt[i // 9, i // 3 % 3, i % 3, y] for i in range(27)]
+        h = collide(f, design[y], node[y])
+        for i in range(27):
+            post[2 * (i // 3 % 3) + y, i // 9, i % 3] = h[i]
+        return carry
+
+    lax.fori_loop(0, 2, collide_first, 0)
+
+    def own(a, b, c, y):
+        return post[2 * b + y, a, c]
+
+    def back(a, b, c, y):
+        return adjoint[2 - a, 2 - b, 2 - c, y]
+
+    pack(own, back, design, node, put_z, put_d)
+
+    plan = [(put_d.at[i], got_d.at[i], 4 + i) for i in range(4)]
+    plan += [(put_z.at[i], got_z.at[i], 2 + i) for i in range(2)]
+    for turn, y in enumerate((1, 0)):
+        plan += [
+            (design.at[y], wide_design.at[3 * turn], turn),
+            (node.at[y], ring_node.at[turn], turn),
         ]
-        sources += [(put_z.at[turn, way], got_z.at[turn, way]) for way in range(2)]
-        sources += [(put_d.at[turn, way], got_d.at[turn, way]) for way in range(4)]
-        copies = [
-            pltpu.make_async_remote_copy(
-                src_ref=src,
-                dst_ref=dst,
-                send_sem=send_sem.at[turn, i],
-                recv_sem=recv_sem.at[turn, i],
-                device_id=near[i],
-                device_id_type=MESH,
-            )
-            for i, (src, dst) in enumerate(sources)
-        ]
-        for copy in reversed(copies):
-            copy.start()
-        return copies
-
-    row = lax.broadcasted_iota(jnp.int32, (8, 128), 0)
-
-    def collide_rows(load, turn):
-        def body(y, carry):
-            f = [load(i, y) for i in range(27)]
-            h = collide(f, design[y], node[y])
-            for i in range(27):
-                post[turn, i // 3 % 3, y, i // 9, i % 3] = h[i]
-            return carry
-
-        lax.fori_loop(0, 2, body, 0)
-
-    def post_tile(turn):
-        return lambda a, b, c, y: post[turn, b, y, a, c]
-
-    def gather(tile, turn, into, flip):
+    plan += [(post.at[pl.ds(3 - 3 * turn, 3)], got_y.at[turn], turn) for turn in range(2)]
+    plan += [(adjoint.at[:, 2 * turn, :, 1 - turn], got_back.at[turn], turn) for turn in range(2)]
+    copies = [
+        pltpu.make_async_remote_copy(
+            src_ref=src,
+            dst_ref=dst,
+            send_sem=send_sem.at[i],
+            recv_sem=recv_sem.at[i],
+            device_id=near[who],
+            device_id_type=MESH,
+        )
+        for i, (src, dst, who) in enumerate(plan)
+    ]
+    pl.semaphore_wait(barrier, len(near))
+    for copy in copies:
+        copy.start()
+    for copy in copies[:12]:
+        copy.wait_recv()
+
+    def outer(a, b, c, y):
+        if 0 <= y < 2:
+            return own(a, b, c, y)
+        turn = 0 if y < 0 else 1
+        return got_y[turn, GROUPS[TURNS[turn]].index((b, y + 2 if y < 0 else y - 2)), a, c]
+
+    def edge_row(kind, a, b, y, way):
+        if 0 <= y < 2:
+            k = 18 * kind + 9 * y + 3 * b + a
+            return got_z[way, k : k + 1, :]
+        turn = 0 if y < 0 else 1
+        j = GROUPS[TURNS[turn]].index((b, y + 2 if y < 0 else y - 2))
+        k = 9 * kind + 3 * j + a
+        return got_d[2 * turn + way, k : k + 1, :]
+
+    def stack_rows(lines):
+        value = jnp.broadcast_to(lines[0], (8, 128))
+        for r in range(1, 8):
+            value = jnp.where(row == r, lines[r], value)
+        return value
+
+    for i in range(27):
+        a, b, c = i // 9, i // 3 % 3, i % 3
+        for t in range(4):
+            y = t - b
+            line = None if c == 1 else edge_row(2, a, b, y, 0 if c == 2 else 1)
+            primal[i, t] = shifted(outer(a, b, c, y), a, c, line, row)
+        lines = []
+        for way in range(2):
+            for t in range(4):
+                y = t - b
+                if c == 1:
+                    lines.append(edge_row(1, a, b, y, way))
+                elif (c == 2) == (way == 0):
+                    lines.append(edge_row(0, a, b, y, way))
+                else:
+                    z = 0 if way == 0 else 7
+                    lines.append(outer(a, b, c, y)[z : z + 1, :])
+        primal[i, 4] = shifted(stack_rows(lines), a, 1, None, row)
+    for y in range(2):
+        wide_design[1 + y] = design[y]
+        wide_node[1 + y] = node[y]
+    for turn in range(2):
+        wide_node[3 * turn] = ring_node[turn]
+    columns = []
+    for part in range(2):
+        lines = []
+        for way in range(2):
+            lines.append(got_d[way, 27 + part : 28 + part, :])
+            for y in range(2):
+                k = CELL_ROW + 2 * y + part
+                lines.append(got_z[way, k : k + 1, :])
+            lines.append(got_d[2 + way, 27 + part : 28 + part, :])
+        columns.append(stack_rows(lines))
+    wide_design[4] = columns[0]
+    one, nought = jnp.ones_like(row), jnp.zeros_like(row)
+    kind = jnp.where(columns[1] == 3.0, one + one + one, nought)
+    kind = jnp.where(columns[1] == 2.0, one + one, kind)
+    wide_node[4] = jnp.where(columns[1] == 1.0, one, kind)
+
+    def collide_second(t, carry):
+        f = [primal[i, t] for i in range(27)]
+        h = collide(f, wide_design[t], wide_node[t])
+        for i in range(27):
+            second[i, t] = h[i]
+        return carry
+
+    lax.fori_loop(0, 5, collide_second, 0)
+
+    for copy in copies[12:]:
+        copy.wait_recv()
+    for i in range(27):
+        a, b, c = i // 9, i // 3 % 3, i % 3
+        way = 0 if c == 2 else 1
         for y in range(2):
-            for i in range(27):
-                a, b, c = i // 9, i // 3 % 3, i % 3
-                value = arrive(
-                    tile, got_y.at[turn], got_z.at[turn], got_d.at[turn], a, b, c, y, row
-                )
-                into[26 - i if flip else i, y] = value
-
-    def adjoint_tile(a, b, c, y):
-        return adjoint[2 - a, 2 - b, 2 - c, y]
-
-    collide_rows(lambda i, y: ckpt[i // 9, i // 3 % 3, i % 3, y], 0)
-    pack(post_tile(0), put_z.at[0], put_d.at[0])
-    pl.semaphore_wait(barrier, len(near))
-    first = sends(0, [post.at[0, 2, 1], post.at[0, 0, 0]])
-    pack(adjoint_tile, put_z.at[2], put_d.at[2])
-    third = sends(2, [adjoint.at[:, 0, :, 1], adjoint.at[:, 2, :, 0]])
-
-    for copy in first:
-        copy.wait_recv()
-    gather(post_tile(0), 0, primal, False)
-
-    collide_rows(lambda i, y: primal[i, y], 1)
-    pack(post_tile(1), put_z.at[1], put_d.at[1])
-    second = sends(1, [post.at[1, 2, 1], post.at[1, 0, 0]])
-
-    for copy in third:
-        copy.wait_recv()
-    gather_adjoint(adjoint_tile, got_y.at[2], got_z.at[2], got_d.at[2], pulled, row)
-
-    for copy in second:
-        copy.wait_recv()
-    gather(post_tile(1), 1, primal, False)
+            t = y - b + 2
+            r = t + 4 * way
+            line = None if c == 1 else second[i, 4, r : r + 1, :]
+            primal[i, y] = shifted(second[i, t], a, c, line, row)
+
+            source = y - (b - 1)
+            if 0 <= source < 2:
+                value = back(a, b, c, source)
+                k = BACK_ROW + 3 * KEPT.index((b, source)) + a if c != 1 else 0
+                line = got_z[way, k : k + 1, :]
+            else:
+                turn = 0 if b == 2 else 1
+                value = got_back[turn, 2 - a, 2 - c]
+                line = got_d[2 * turn + way, 29 + a : 30 + a, :]
+            pulled[26 - i, y] = shifted(value, a, c, line, row)
 
     def backward(y, carry):
         f = [primal[i, y] for i in range(27)]
@@ -276,25 +368,8 @@
         return carry
 
     lax.fori_loop(0, 2, backward, 0)
-    for copy in first + third + second:
+    for copy in copies:
         copy.wait_send()
-
-
-class Reversed:
-    def __init__(self, ref):
-        self.ref = ref
-
-    def __getitem__(self, key):
-        turn, a, c = key
-        return self.ref[turn, 2 - a, 2 - c]
-
-
-def gather_adjoint(tile, got_y, got_z, got_d, into, row):
-    for y in range(2):
-        for i in range(27):
-            a, b, c = i // 9, i // 3 % 3, i % 3
-            value = arrive(tile, Reversed(got_y), got_z, got_d, a, b, c, y, row)
-            into[26 - i, y] = value
 
 
 def solution(mesh):
@@ -313,16 +388,21 @@
             in_specs=[whole] * 4,
             out_specs=(whole, whole),
             scratch_shapes=[
-                pltpu.VMEM((2, 3, 2, 3, 3, 8, 128), f32),
+                pltpu.VMEM((6, 3, 3, 8, 128), f32),
+                pltpu.VMEM((27, 5, 8, 128), f32),
+                pltpu.VMEM((5, 8, 128), f32),
+                pltpu.VMEM((5, 8, 128), jnp.int32),
+                pltpu.VMEM((2, 8, 128), jnp.int32),
+                pltpu.VMEM((27, 5, 8, 128), f32),
                 pltpu.VMEM((27, 2, 8, 128), f32),
-                pltpu.VMEM((27, 2, 8, 128), f32),
-                pltpu.VMEM((3, 2, 3, 3, 8, 128), f32),
-                pltpu.VMEM((3, 2, 16, 128), f32),
-                pltpu.VMEM((3, 2, 16, 128), f32),
-                pltpu.VMEM((3, 4, 8, 128), f32),
-                pltpu.VMEM((3, 4, 8, 128), f32),
-                pltpu.SemaphoreType.DMA((3, 8)),
-                pltpu.SemaphoreType.DMA((3, 8)),
+                pltpu.VMEM((2, 3, 3, 3, 8, 128), f32),
+                pltpu.VMEM((2, 3, 3, 8, 128), f32),
+                pltpu.VMEM((2, 72, 128), f32),
+                pltpu.VMEM((2, 72, 128), f32),
+                pltpu.VMEM((4, 32, 128), f32),
+                pltpu.VMEM((4, 32, 128), f32),
+                pltpu.SemaphoreType.DMA((14,)),
+                pltpu.SemaphoreType.DMA((14,)),
             ],
             compiler_params=pltpu.CompilerParams(collective_id=0, has_side_effects=True),
             name="adjoint_step",

time: 32.6 us -> 26.8 us (0.82)
  the two profiles are of different devices: /device:TPU:8 before, /device:TPU:6 now
where the time goes in v2:
time: 26.8 us; the launch traced here: 26.7 us
  Pallas kernels  23.8 us (89%)
  local copies, waits for them, and re-layouts  2.24 us (8%)
  between operations  0.65 us (2%)
    pallas_call x1, Pallas kernels, local(): pl.pallas_call(lambda *refs: kernel(counts, *refs), out_shape=(jax.ShapeD...  23.8 us
    unnamed x4, local copies, waits for them, and re-layouts  2.24 us

profile of v2, /device:TPU:6, one launch (start us, length us, event | category | flops | bytes accessed | tf_op | source)
XLA Modules:
  0.0 26.7 jit_solution(15764104804246216753)
XLA Ops:
  0.6 23.8 %adjoint_step.1 = (f32[3,3,3,2,8,128]{5,4,3,2,1,0:T(8,128)}, f32[2,8,128]{2,1,0:T(8,128)}) custom-call(f32[3,3,3,2,8,128]{5,4,3,2,1,0:T(8,128)} %bitcast.3, f32[3,3,3,2,8,128]{5,4,3,2,1,0:T(8,128)} %bitcast.4, f32[2,8,128]{2,1,0:T(8,128)} %refs_2_.1, s32[2,8,128]{2,1,0:T(8,128)} %refs_3_.1), custom_call_target="tpu_custom_call" | custom-call | tf_op jit(solution)/shard_map/adjoint_step/pallas_call | solution.py:382
  24.4 0.0 copy-start
  24.4 1.6 %copy.8 = f32[27,2,8,128]{3,2,1,0:T(8,128)} copy(f32[27,2,8,128]{3,2,1,0:T(8,128)} %bitcast.5) | data formatting | bytes 442368
  26.1 0.0 copy-done
  26.1 0.6 %copy.9 = f32[2,8,128]{2,1,0:T(8,128)} copy(f32[2,8,128]{2,1,0:T(8,128)S(1)} %copy-done) | data formatting | bytes 16384
Async XLA Ops:
  24.4 1.7 %copy-start = (f32[2,8,128]{2,1,0:T(8,128)S(1)}, f32[2,8,128]{2,1,0:T(8,128)}, u32[]{:S(2)}) copy-start(f32[2,8,128]{2,1,0:T(8,128)} %get-tuple-element.9) | copy-start | bytes 24580

commit v3 on v2

--- a/solution.py
+++ b/solution.py
@@ -156,8 +156,8 @@
                         rows_z[way, k : k + 1, :] = tile(a, b, c, y)[z : z + 1, :]
         for y in range(2):
             k = CELL_ROW + 2 * y
-            rows_z[way, k : k + 1, :] = design[y, near : near + 1, :]
-            rows_z[way, k + 1 : k + 2, :] = node[y, near : near + 1, :].astype(jnp.float32)
+            rows_z[way, k : k + 1, :] = design[1 + y, near : near + 1, :]
+            rows_z[way, k + 1 : k + 2, :] = node[1 + y, near : near + 1, :].astype(jnp.float32)
         for k, (b, y) in enumerate(KEPT):
             for a in range(3):
                 at = BACK_ROW + 3 * k + a
@@ -171,8 +171,8 @@
                         k = 9 * kind + 3 * j + a
                         rows_d[corner, k : k + 1, :] = tile(a, b, c, y)[z : z + 1, :]
             y = edge(step_y, 1)
-            rows_d[corner, 27:28, :] = design[y, near : near + 1, :]
-            rows_d[corner, 28:29, :] = node[y, near : near + 1, :].astype(jnp.float32)
+            rows_d[corner, 27:28, :] = design[1 + y, near : near + 1, :]
+            rows_d[corner, 28:29, :] = node[1 + y, near : near + 1, :].astype(jnp.float32)
             for a in range(3):
                 rows_d[corner, 29 + a : 30 + a, :] = back(a, 1 + step_y, 1 + step, y)[
                     near : near + 1, :
@@ -188,27 +188,30 @@
     return value
 
 
-def kernel(
+def gather_kernel(
     counts,
+    ckpt_in,
+    adjoint_in,
+    design_in,
+    node_in,
+    final,
+    pulled,
+    design_out,
+    node_out,
     ckpt,
     adjoint,
-    design,
-    node,
-    previous,
-    sensitivity,
     post,
     primal,
     wide_design,
     wide_node,
-    ring_node,
     second,
-    pulled,
     got_y,
     got_back,
     put_z,
     got_z,
     put_d,
     got_d,
+    load_sem,
     send_sem,
     recv_sem,
 ):
@@ -221,11 +224,26 @@
     for who in near:
         pl.semaphore_signal(barrier, inc=1, device_id=who, device_id_type=MESH)
 
+    loads = [
+        pltpu.make_async_copy(src, dst, load_sem.at[i])
+        for i, (src, dst) in enumerate(
+            [
+                (ckpt_in, ckpt),
+                (design_in, wide_design.at[pl.ds(1, 2)]),
+                (node_in, wide_node.at[pl.ds(1, 2)]),
+                (adjoint_in, adjoint),
+            ]
+        )
+    ]
+    for load in loads:
+        load.start()
     row = lax.broadcasted_iota(jnp.int32, (8, 128), 0)
+    for load in loads[:3]:
+        load.wait()
 
     def collide_first(y, carry):
         f = [ckpt[i // 9, i // 3 % 3, i % 3, y] for i in range(27)]
-        h = collide(f, design[y], node[y])
+        h = collide(f, wide_design[1 + y], wide_node[1 + y])
         for i in range(27):
             post[2 * (i // 3 % 3) + y, i // 9, i % 3] = h[i]
         return carry
@@ -238,14 +256,15 @@
     def back(a, b, c, y):
         return adjoint[2 - a, 2 - b, 2 - c, y]
 
-    pack(own, back, design, node, put_z, put_d)
+    loads[3].wait()
+    pack(own, back, wide_design, wide_node, put_z, put_d)
 
     plan = [(put_d.at[i], got_d.at[i], 4 + i) for i in range(4)]
     plan += [(put_z.at[i], got_z.at[i], 2 + i) for i in range(2)]
     for turn, y in enumerate((1, 0)):
         plan += [
-            (design.at[y], wide_design.at[3 * turn], turn),
-            (node.at[y], ring_node.at[turn], turn),
+            (wide_design.at[1 + y], wide_design.at[3 * turn], turn),
+            (wide_node.at[1 + y], wide_node.at[3 * turn], turn),
         ]
     plan += [(post.at[pl.ds(3 - 3 * turn, 3)], got_y.at[turn], turn) for turn in range(2)]
     plan += [(adjoint.at[:, 2 * turn, :, 1 - turn], got_back.at[turn], turn) for turn in range(2)]
@@ -305,11 +324,6 @@
                     z = 0 if way == 0 else 7
                     lines.append(outer(a, b, c, y)[z : z + 1, :])
         primal[i, 4] = shifted(stack_rows(lines), a, 1, None, row)
-    for y in range(2):
-        wide_design[1 + y] = design[y]
-        wide_node[1 + y] = node[y]
-    for turn in range(2):
-        wide_node[3 * turn] = ring_node[turn]
     columns = []
     for part in range(2):
         lines = []
@@ -344,7 +358,7 @@
             t = y - b + 2
             r = t + 4 * way
             line = None if c == 1 else second[i, 4, r : r + 1, :]
-            primal[i, y] = shifted(second[i, t], a, c, line, row)
+            final[i, y] = shifted(second[i, t], a, c, line, row)
 
             source = y - (b - 1)
             if 0 <= source < 2:
@@ -357,19 +371,28 @@
                 line = got_d[2 * turn + way, 29 + a : 30 + a, :]
             pulled[26 - i, y] = shifted(value, a, c, line, row)
 
-    def backward(y, carry):
-        f = [primal[i, y] for i in range(27)]
-        kind = node[y]
-        _, pull = jax.vjp(lambda pops, field: collide(pops, field, kind), f, design[y])
-        grads, slope = pull([pulled[i, y] for i in range(27)])
-        for i in range(27):
-            previous[i // 9, i // 3 % 3, i % 3, y] = grads[i]
-        sensitivity[y] = slope
-        return carry
-
-    lax.fori_loop(0, 2, backward, 0)
+    for y in range(2):
+        design_out[y] = wide_design[1 + y]
+        node_out[y] = wide_node[1 + y]
     for copy in copies:
         copy.wait_send()
+
+
+def backward_kernel(final, pulled, design, node, previous, sensitivity, grads, slopes, sem):
+    copies = []
+    for y in range(2):
+        f = [final[i, y] for i in range(27)]
+        kind = node[y]
+        _, pull = jax.vjp(lambda pops, field, kind=kind: collide(pops, field, kind), f, design[y])
+        values, slopes[y] = pull([pulled[i, y] for i in range(27)])
+        for i in range(27):
+            grads[y, i] = values[i]
+        copies.append(pltpu.make_async_copy(grads.at[y], previous.at[:, y], sem.at[y]))
+        copies[-1].start()
+    copies.append(pltpu.make_async_copy(slopes, sensitivity, sem.at[2]))
+    copies[-1].start()
+    for copy in copies:
+        copy.wait()
 
 
 def solution(mesh):
@@ -378,41 +401,68 @@
     def local(ckpt_pops, adjoint_pops, design, node_types):
         f32 = jnp.float32
         cells = ckpt_pops.shape[1:]
-        whole = pl.BlockSpec(memory_space=pltpu.VMEM)
-        previous, sensitivity = pl.pallas_call(
-            lambda *refs: kernel(counts, *refs),
+        hbm = pl.BlockSpec(memory_space=pltpu.HBM)
+        vmem = pl.BlockSpec(memory_space=pltpu.VMEM)
+        slabs = (27,) + cells
+        gathered = pl.pallas_call(
+            lambda *refs: gather_kernel(counts, *refs),
             out_shape=(
-                jax.ShapeDtypeStruct((3, 3, 3) + cells, f32),
-                jax.ShapeDtypeStruct(cells, f32),
+                pltpu.VMEM(slabs, f32),
+                pltpu.VMEM(slabs, f32),
+                pltpu.VMEM(cells, f32),
+                pltpu.VMEM(cells, jnp.int32),
             ),
-            in_specs=[whole] * 4,
-            out_specs=(whole, whole),
+            in_specs=[hbm] * 4,
+            out_specs=[vmem] * 4,
             scratch_shapes=[
+                pltpu.VMEM((3, 3, 3) + cells, f32),
+                pltpu.VMEM((3, 3, 3) + cells, f32),
                 pltpu.VMEM((6, 3, 3, 8, 128), f32),
                 pltpu.VMEM((27, 5, 8, 128), f32),
                 pltpu.VMEM((5, 8, 128), f32),
                 pltpu.VMEM((5, 8, 128), jnp.int32),
-                pltpu.VMEM((2, 8, 128), jnp.int32),
                 pltpu.VMEM((27, 5, 8, 128), f32),
-                pltpu.VMEM((27, 2, 8, 128), f32),
                 pltpu.VMEM((2, 3, 3, 3, 8, 128), f32),
                 pltpu.VMEM((2, 3, 3, 8, 128), f32),
                 pltpu.VMEM((2, 72, 128), f32),
                 pltpu.VMEM((2, 72, 128), f32),
                 pltpu.VMEM((4, 32, 128), f32),
                 pltpu.VMEM((4, 32, 128), f32),
+                pltpu.SemaphoreType.DMA((4,)),
                 pltpu.SemaphoreType.DMA((14,)),
                 pltpu.SemaphoreType.DMA((14,)),
             ],
-            compiler_params=pltpu.CompilerParams(collective_id=0, has_side_effects=True),
-            name="adjoint_step",
+            compiler_params=pltpu.CompilerParams(
+                collective_id=0, has_side_effects=True, vmem_limit_bytes=16 * 2**20
+            ),
+            name="gather_cells",
         )(
-            ckpt_pops.reshape((3, 3, 3) + cells),
-            adjoint_pops.reshape((3, 3, 3) + cells),
-            design,
-            node_types,
+            *[
+                pltpu.with_memory_space_constraint(array, pltpu.HBM)
+                for array in (
+                    ckpt_pops.reshape((3, 3, 3) + cells),
+                    adjoint_pops.reshape((3, 3, 3) + cells),
+                    design,
+                    node_types,
+                )
+            ]
         )
-        return previous.reshape(ckpt_pops.shape), sensitivity
+        return pl.pallas_call(
+            backward_kernel,
+            out_shape=(
+                jax.ShapeDtypeStruct(slabs, f32),
+                jax.ShapeDtypeStruct(cells, f32),
+            ),
+            in_specs=[vmem] * 4,
+            out_specs=[hbm] * 2,
+            scratch_shapes=[
+                pltpu.VMEM((2, 27, 8, 128), f32),
+                pltpu.VMEM((2, 8, 128), f32),
+                pltpu.SemaphoreType.DMA((3,)),
+            ],
+            compiler_params=pltpu.CompilerParams(vmem_limit_bytes=16 * 2**20),
+            name="backward_cells",
+        )(*gathered)
 
     return jax.shard_map(
         local,

time: 26.8 us -> 23.6 us (0.88)
  local copies, waits for them, and re-layouts: 2.24 us -> 0 us
  Pallas kernels: 23.8 us -> 22.8 us
    unnamed x4 -> x0, local copies, waits for them, and re-layouts: 2.24 us -> none
    pallas_call x1 -> x2, Pallas kernels: 23.8 us -> 22.8 us  [the longest x1 21.8 us: local(): pl.pallas_call(lambda *refs: gather_kernel(counts, *refs), out_shape=(plt...]
where the time goes in v3:
time: 23.6 us; the launch traced here: 23.4 us
  Pallas kernels  22.8 us (97%)
  between operations  0.64 us (3%)
    pallas_call x1, Pallas kernels, local(): pl.pallas_call(lambda *refs: gather_kernel(counts, *refs), out_shape=(plt...  21.8 us
    pallas_call x1, Pallas kernels, local(): pl.pallas_call(backward_kernel, out_shape=(jax.ShapeDtypeStruct(slabs, f3...  0.96 us

profile of v3, /device:TPU:6, one launch (start us, length us, event | category | flops | bytes accessed | tf_op | source)
XLA Modules:
  0.0 23.4 jit_solution(14821497683233585480)
XLA Ops:
  0.6 21.8 %gather_cells.1 = (f32[27,2,8,128]{3,2,1,0:T(8,128)S(1)}, f32[27,2,8,128]{3,2,1,0:T(8,128)S(1)}, f32[2,8,128]{2,1,0:T(8,128)S(1)}, s32[2,8,128]{2,1,0:T(8,128)S(1)}) custom-call(f32[3,3,3,2,8,128]{5,4,3,2,1,0:T(8,128)} %bitcast.2, f32[3,3,3,2,8,128]{5,4,3,2,1,0:T(8,128)} %bitcast.3, f32[2,8,128]{2,1,0:T(8,128)} %refs_2_.1, s32[2,8,128]{2,1,0:T(8,128)} %refs_3_.1), custom_call_target="tpu_custom_call" | custom-call | tf_op jit(solution)/shard_map/gather_cells/pallas_call | solution.py:407
  22.5 1.0 %backward_cells.1 = (f32[27,2,8,128]{3,2,1,0:T(8,128)}, f32[2,8,128]{2,1,0:T(8,128)}) custom-call(f32[27,2,8,128]{3,2,1,0:T(8,128)S(1)} %get-tuple-element.6.final, f32[27,2,8,128]{3,2,1,0:T(8,128)S(1)} %get-tuple-element.7.pulled, f32[2,8,128]{2,1,0:T(8,128)S(1)} %get-tuple-element.8.design, s32[2,8,128]{2,1,0:T(8,128)S(1)} %get-tuple-element.9.node), custom_call_target="tpu_custom_call" | custom-call | tf_op jit(solution)/shard_map/backward_cells/pallas_call | solution.py:450

commit v4 on v3

--- a/solution.py
+++ b/solution.py
@@ -10,7 +10,7 @@
 inflow = 0.05
 
 MESH = pl.DeviceIdType.MESH
-SIDES = [(1, 0), (-1, 0), (0, 1), (0, -1), (1, 1), (1, -1), (-1, 1), (-1, -1)]
+SIDES = [(1, 0), (-1, 0), (0, 1), (0, -1)]
 
 
 def full(like, value):
@@ -134,7 +134,7 @@
 
 
 GROUPS = {1: [(1, 1), (2, 0), (2, 1)], -1: [(0, 0), (0, 1), (1, 0)]}
-CELL_ROW, BACK_ROW = 54, 58
+BACK_ROW = 64
 KEPT = [(1, 0), (1, 1), (2, 0), (0, 1)]
 TURNS = (1, -1)
 
@@ -144,39 +144,27 @@
     return [(far, 1 + step), (near, 1), (near, 1 + step)][kind]
 
 
-def pack(tile, back, design, node, rows_z, rows_d):
+def pack(tile, back, design, node, rows):
     for way, step in enumerate(TURNS):
         near = edge(step, 7)
-        for kind in range(3):
-            z, c = moving(step, kind)
-            for y in range(2):
-                for b in range(3):
-                    for a in range(3):
-                        k = 18 * kind + 9 * y + 3 * b + a
-                        rows_z[way, k : k + 1, :] = tile(a, b, c, y)[z : z + 1, :]
-        for y in range(2):
-            k = CELL_ROW + 2 * y
-            rows_z[way, k : k + 1, :] = design[1 + y, near : near + 1, :]
-            rows_z[way, k + 1 : k + 2, :] = node[1 + y, near : near + 1, :].astype(jnp.float32)
-        for k, (b, y) in enumerate(KEPT):
-            for a in range(3):
-                at = BACK_ROW + 3 * k + a
-                rows_z[way, at : at + 1, :] = back(a, b, 1 + step, y)[near : near + 1, :]
         for turn, step_y in enumerate(TURNS):
-            corner = 2 * turn + way
+            base = 32 * turn
             for kind in range(3):
                 z, c = moving(step, kind)
                 for j, (b, y) in enumerate(GROUPS[step_y]):
                     for a in range(3):
-                        k = 9 * kind + 3 * j + a
-                        rows_d[corner, k : k + 1, :] = tile(a, b, c, y)[z : z + 1, :]
-            y = edge(step_y, 1)
-            rows_d[corner, 27:28, :] = design[1 + y, near : near + 1, :]
-            rows_d[corner, 28:29, :] = node[1 + y, near : near + 1, :].astype(jnp.float32)
+                        k = base + 9 * kind + 3 * j + a
+                        rows[way, k : k + 1, :] = tile(a, b, c, y)[z : z + 1, :]
+            y, k = edge(step_y, 1), base + 27
+            rows[way, k : k + 1, :] = design[1 + y, near : near + 1, :]
+            rows[way, k + 1 : k + 2, :] = node[1 + y, near : near + 1, :].astype(jnp.float32)
             for a in range(3):
-                rows_d[corner, 29 + a : 30 + a, :] = back(a, 1 + step_y, 1 + step, y)[
-                    near : near + 1, :
-                ]
+                k = base + 29 + a
+                rows[way, k : k + 1, :] = back(a, 1 + step_y, 1 + step, y)[near : near + 1, :]
+        for j, (b, y) in enumerate(KEPT):
+            for a in range(3):
+                k = BACK_ROW + 3 * j + a
+                rows[way, k : k + 1, :] = back(a, b, 1 + step, y)[near : near + 1, :]
 
 
 def shifted(value, a, c, line, row):
@@ -209,7 +197,6 @@
     got_back,
     put_z,
     got_z,
-    put_d,
     got_d,
     load_sem,
     send_sem,
@@ -257,10 +244,9 @@
         return adjoint[2 - a, 2 - b, 2 - c, y]
 
     loads[3].wait()
-    pack(own, back, wide_design, wide_node, put_z, put_d)
-
-    plan = [(put_d.at[i], got_d.at[i], 4 + i) for i in range(4)]
-    plan += [(put_z.at[i], got_z.at[i], 2 + i) for i in range(2)]
+    pack(own, back, wide_design, wide_node, put_z)
+
+    plan = [(put_z.at[i], got_z.at[i], 2 + i) for i in range(2)]
     for turn, y in enumerate((1, 0)):
         plan += [
             (wide_design.at[1 + y], wide_design.at[3 * turn], turn),
@@ -268,6 +254,11 @@
         ]
     plan += [(post.at[pl.ds(3 - 3 * turn, 3)], got_y.at[turn], turn) for turn in range(2)]
     plan += [(adjoint.at[:, 2 * turn, :, 1 - turn], got_back.at[turn], turn) for turn in range(2)]
+    plan += [
+        (got_z.at[way, pl.ds(32 * turn, 32)], got_d.at[2 * turn + way], turn)
+        for way in range(2)
+        for turn in range(2)
+    ]
     copies = [
         pltpu.make_async_remote_copy(
             src_ref=src,
@@ -280,9 +271,13 @@
         for i, (src, dst, who) in enumerate(plan)
     ]
     pl.semaphore_wait(barrier, len(near))
-    for copy in copies:
+    for copy in copies[:10]:
         copy.start()
-    for copy in copies[:12]:
+    for way in range(2):
+        copies[way].wait_recv()
+        for copy in copies[10 + 2 * way : 12 + 2 * way]:
+            copy.start()
+    for copy in copies[2:8] + copies[10:]:
         copy.wait_recv()
 
     def outer(a, b, c, y):
@@ -292,12 +287,11 @@
         return got_y[turn, GROUPS[TURNS[turn]].index((b, y + 2 if y < 0 else y - 2)), a, c]
 
     def edge_row(kind, a, b, y, way):
+        turn = 0 if y < 0 or y < 2 and (b, y) in GROUPS[1] else 1
+        j = GROUPS[TURNS[turn]].index((b, y % 2))
+        k = 9 * kind + 3 * j + a
         if 0 <= y < 2:
-            k = 18 * kind + 9 * y + 3 * b + a
-            return got_z[way, k : k + 1, :]
-        turn = 0 if y < 0 else 1
-        j = GROUPS[TURNS[turn]].index((b, y + 2 if y < 0 else y - 2))
-        k = 9 * kind + 3 * j + a
+            return got_z[way, 32 * turn + k : 32 * turn + k + 1, :]
         return got_d[2 * turn + way, k : k + 1, :]
 
     def stack_rows(lines):
@@ -330,7 +324,7 @@
         for way in range(2):
             lines.append(got_d[way, 27 + part : 28 + part, :])
             for y in range(2):
-                k = CELL_ROW + 2 * y + part
+                k = 32 * (1 - y) + 27 + part
                 lines.append(got_z[way, k : k + 1, :])
             lines.append(got_d[2 + way, 27 + part : 28 + part, :])
         columns.append(stack_rows(lines))
@@ -349,7 +343,7 @@
 
     lax.fori_loop(0, 5, collide_second, 0)
 
-    for copy in copies[12:]:
+    for copy in copies[8:10]:
         copy.wait_recv()
     for i in range(27):
         a, b, c = i // 9, i // 3 % 3, i % 3
@@ -424,9 +418,8 @@
                 pltpu.VMEM((27, 5, 8, 128), f32),
                 pltpu.VMEM((2, 3, 3, 3, 8, 128), f32),
                 pltpu.VMEM((2, 3, 3, 8, 128), f32),
-                pltpu.VMEM((2, 72, 128), f32),
-                pltpu.VMEM((2, 72, 128), f32),
-                pltpu.VMEM((4, 32, 128), f32),
+                pltpu.VMEM((2, 80, 128), f32),
+                pltpu.VMEM((2, 80, 128), f32),
                 pltpu.VMEM((4, 32, 128), f32),
                 pltpu.SemaphoreType.DMA((4,)),
                 pltpu.SemaphoreType.DMA((14,)),

time: 23.6 us -> 23.9 us (1.013)
  the two profiles are of different devices: /device:TPU:6 before, /device:TPU:59 now
where the time goes in v4:
time: 23.9 us; the launch traced here: 23.8 us
  Pallas kernels  23.2 us (97%)
  between operations  0.64 us (3%)
    pallas_call x1, Pallas kernels, local(): pl.pallas_call(lambda *refs: gather_kernel(counts, *refs), out_shape=(plt...  22.2 us
    pallas_call x1, Pallas kernels, local(): pl.pallas_call(backward_kernel, out_shape=(jax.ShapeDtypeStruct(slabs, f3...  0.96 us

profile of v4, /device:TPU:59, one launch (start us, length us, event | category | flops | bytes accessed | tf_op | source)
XLA Modules:
  0.0 23.8 jit_solution(14589588262686830214)
XLA Ops:
  0.6 22.2 %gather_cells.1 = (f32[27,2,8,128]{3,2,1,0:T(8,128)S(1)}, f32[27,2,8,128]{3,2,1,0:T(8,128)S(1)}, f32[2,8,128]{2,1,0:T(8,128)S(1)}, s32[2,8,128]{2,1,0:T(8,128)S(1)}) custom-call(f32[3,3,3,2,8,128]{5,4,3,2,1,0:T(8,128)} %bitcast.2, f32[3,3,3,2,8,128]{5,4,3,2,1,0:T(8,128)} %bitcast.3, f32[2,8,128]{2,1,0:T(8,128)} %refs_2_.1, s32[2,8,128]{2,1,0:T(8,128)} %refs_3_.1), custom_call_target="tpu_custom_call" | custom-call | tf_op jit(solution)/shard_map/gather_cells/pallas_call | solution.py:401
  22.8 1.0 %backward_cells.1 = (f32[27,2,8,128]{3,2,1,0:T(8,128)}, f32[2,8,128]{2,1,0:T(8,128)}) custom-call(f32[27,2,8,128]{3,2,1,0:T(8,128)S(1)} %get-tuple-element.6.final, f32[27,2,8,128]{3,2,1,0:T(8,128)S(1)} %get-tuple-element.7.pulled, f32[2,8,128]{2,1,0:T(8,128)S(1)} %get-tuple-element.8.design, s32[2,8,128]{2,1,0:T(8,128)S(1)} %get-tuple-element.9.node), custom_call_target="tpu_custom_call" | custom-call | tf_op jit(solution)/shard_map/backward_cells/pallas_call | solution.py:443

commit v5 on v4

--- a/solution.py
+++ b/solution.py
@@ -246,7 +246,9 @@
     loads[3].wait()
     pack(own, back, wide_design, wide_node, put_z)
 
-    plan = [(put_z.at[i], got_z.at[i], 2 + i) for i in range(2)]
+    parts = [(way, pl.ds(32 * turn, 32), turn) for way in range(2) for turn in range(2)]
+    stay = pl.ds(BACK_ROW, 16)
+    plan = [(put_z.at[way, part], got_z.at[way, part], 2 + way) for way, part, _ in parts]
     for turn, y in enumerate((1, 0)):
         plan += [
             (wide_design.at[1 + y], wide_design.at[3 * turn], turn),
@@ -254,11 +256,8 @@
         ]
     plan += [(post.at[pl.ds(3 - 3 * turn, 3)], got_y.at[turn], turn) for turn in range(2)]
     plan += [(adjoint.at[:, 2 * turn, :, 1 - turn], got_back.at[turn], turn) for turn in range(2)]
-    plan += [
-        (got_z.at[way, pl.ds(32 * turn, 32)], got_d.at[2 * turn + way], turn)
-        for way in range(2)
-        for turn in range(2)
-    ]
+    plan += [(put_z.at[way, stay], got_z.at[way, stay], 2 + way) for way in range(2)]
+    plan += [(got_z.at[way, part], got_d.at[2 * turn + way], turn) for way, part, turn in parts]
     copies = [
         pltpu.make_async_remote_copy(
             src_ref=src,
@@ -271,13 +270,12 @@
         for i, (src, dst, who) in enumerate(plan)
     ]
     pl.semaphore_wait(barrier, len(near))
-    for copy in copies[:10]:
+    for copy in copies[:14]:
         copy.start()
-    for way in range(2):
-        copies[way].wait_recv()
-        for copy in copies[10 + 2 * way : 12 + 2 * way]:
-            copy.start()
-    for copy in copies[2:8] + copies[10:]:
+    for k in range(4):
+        copies[k].wait_recv()
+        copies[14 + k].start()
+    for copy in copies[4:10] + copies[14:]:
         copy.wait_recv()
 
     def outer(a, b, c, y):
@@ -343,7 +341,7 @@
 
     lax.fori_loop(0, 5, collide_second, 0)
 
-    for copy in copies[8:10]:
+    for copy in copies[10:14]:
         copy.wait_recv()
     for i in range(27):
         a, b, c = i // 9, i // 3 % 3, i % 3
@@ -422,8 +420,8 @@
                 pltpu.VMEM((2, 80, 128), f32),
                 pltpu.VMEM((4, 32, 128), f32),
                 pltpu.SemaphoreType.DMA((4,)),
-                pltpu.SemaphoreType.DMA((14,)),
-                pltpu.SemaphoreType.DMA((14,)),
+                pltpu.SemaphoreType.DMA((18,)),
+                pltpu.SemaphoreType.DMA((18,)),
             ],
             compiler_params=pltpu.CompilerParams(
                 collective_id=0, has_side_effects=True, vmem_limit_bytes=16 * 2**20

time: 23.9 us -> 23.8 us (level)
  no operation moved by 1% of the time
where the time goes in v5:
time: 23.8 us; the launch traced here: 23.7 us
  Pallas kernels  23.1 us (97%)
  between operations  0.64 us (3%)
    pallas_call x1, Pallas kernels, local(): pl.pallas_call(lambda *refs: gather_kernel(counts, *refs), out_shape=(plt...  22.1 us
    pallas_call x1, Pallas kernels, local(): pl.pallas_call(backward_kernel, out_shape=(jax.ShapeDtypeStruct(slabs, f3...  0.96 us

profile of v5, /device:TPU:59, one launch (start us, length us, event | category | flops | bytes accessed | tf_op | source)
XLA Modules:
  0.0 23.7 jit_solution(16200426532595962023)
XLA Ops:
  0.6 22.1 %gather_cells.1 = (f32[27,2,8,128]{3,2,1,0:T(8,128)S(1)}, f32[27,2,8,128]{3,2,1,0:T(8,128)S(1)}, f32[2,8,128]{2,1,0:T(8,128)S(1)}, s32[2,8,128]{2,1,0:T(8,128)S(1)}) custom-call(f32[3,3,3,2,8,128]{5,4,3,2,1,0:T(8,128)} %bitcast.2, f32[3,3,3,2,8,128]{5,4,3,2,1,0:T(8,128)} %bitcast.3, f32[2,8,128]{2,1,0:T(8,128)} %refs_2_.1, s32[2,8,128]{2,1,0:T(8,128)} %refs_3_.1), custom_call_target="tpu_custom_call" | custom-call | tf_op jit(solution)/shard_map/gather_cells/pallas_call | solution.py:399
  22.7 1.0 %backward_cells.1 = (f32[27,2,8,128]{3,2,1,0:T(8,128)}, f32[2,8,128]{2,1,0:T(8,128)}) custom-call(f32[27,2,8,128]{3,2,1,0:T(8,128)S(1)} %get-tuple-element.6.final, f32[27,2,8,128]{3,2,1,0:T(8,128)S(1)} %get-tuple-element.7.pulled, f32[2,8,128]{2,1,0:T(8,128)S(1)} %get-tuple-element.8.design, s32[2,8,128]{2,1,0:T(8,128)S(1)} %get-tuple-element.9.node), custom_call_target="tpu_custom_call" | custom-call | tf_op jit(solution)/shard_map/backward_cells/pallas_call | solution.py:441

commit v6 on v3

--- a/solution.py
+++ b/solution.py
@@ -260,13 +260,13 @@
     pack(own, back, wide_design, wide_node, put_z, put_d)
 
     plan = [(put_d.at[i], got_d.at[i], 4 + i) for i in range(4)]
-    plan += [(put_z.at[i], got_z.at[i], 2 + i) for i in range(2)]
+    plan += [(post.at[pl.ds(3 - 3 * turn, 3)], got_y.at[turn], turn) for turn in range(2)]
     for turn, y in enumerate((1, 0)):
         plan += [
             (wide_design.at[1 + y], wide_design.at[3 * turn], turn),
             (wide_node.at[1 + y], wide_node.at[3 * turn], turn),
         ]
-    plan += [(post.at[pl.ds(3 - 3 * turn, 3)], got_y.at[turn], turn) for turn in range(2)]
+    plan += [(put_z.at[i], got_z.at[i], 2 + i) for i in range(2)]
     plan += [(adjoint.at[:, 2 * turn, :, 1 - turn], got_back.at[turn], turn) for turn in range(2)]
     copies = [
         pltpu.make_async_remote_copy(

time: 23.6 us -> 23.4 us (level)
  no operation moved by 1% of the time
where the time goes in v6:
time: 23.4 us; the launch traced here: 23.3 us
  Pallas kernels  22.7 us (97%)
  between operations  0.64 us (3%)
    pallas_call x1, Pallas kernels, local(): pl.pallas_call(lambda *refs: gather_kernel(counts, *refs), out_shape=(plt...  21.7 us
    pallas_call x1, Pallas kernels, local(): pl.pallas_call(backward_kernel, out_shape=(jax.ShapeDtypeStruct(slabs, f3...  0.96 us

profile of v6, /device:TPU:6, one launch (start us, length us, event | category | flops | bytes accessed | tf_op | source)
XLA Modules:
  0.0 23.3 jit_solution(6520266549797274612)
XLA Ops:
  0.6 21.7 %gather_cells.1 = (f32[27,2,8,128]{3,2,1,0:T(8,128)S(1)}, f32[27,2,8,128]{3,2,1,0:T(8,128)S(1)}, f32[2,8,128]{2,1,0:T(8,128)S(1)}, s32[2,8,128]{2,1,0:T(8,128)S(1)}) custom-call(f32[3,3,3,2,8,128]{5,4,3,2,1,0:T(8,128)} %bitcast.2, f32[3,3,3,2,8,128]{5,4,3,2,1,0:T(8,128)} %bitcast.3, f32[2,8,128]{2,1,0:T(8,128)} %refs_2_.1, s32[2,8,128]{2,1,0:T(8,128)} %refs_3_.1), custom_call_target="tpu_custom_call" | custom-call | tf_op jit(solution)/shard_map/gather_cells/pallas_call | solution.py:407
  22.3 1.0 %backward_cells.1 = (f32[27,2,8,128]{3,2,1,0:T(8,128)}, f32[2,8,128]{2,1,0:T(8,128)}) custom-call(f32[27,2,8,128]{3,2,1,0:T(8,128)S(1)} %get-tuple-element.6.final, f32[27,2,8,128]{3,2,1,0:T(8,128)S(1)} %get-tuple-element.7.pulled, f32[2,8,128]{2,1,0:T(8,128)S(1)} %get-tuple-element.8.design, s32[2,8,128]{2,1,0:T(8,128)S(1)} %get-tuple-element.9.node), custom_call_target="tpu_custom_call" | custom-call | tf_op jit(solution)/shard_map/backward_cells/pallas_call | solution.py:450

commit v7 on v6

--- a/solution.py
+++ b/solution.py
@@ -221,7 +221,7 @@
         for dy, dz in SIDES
     ]
     barrier = pltpu.get_barrier_semaphore()
-    for who in near:
+    for who in reversed(near):
         pl.semaphore_signal(barrier, inc=1, device_id=who, device_id_type=MESH)
 
     loads = [

time: 23.4 us -> 23.4 us (level)
  no operation moved by 1% of the time
where the time goes in v7:
time: 23.4 us; the launch traced here: 23.3 us
  Pallas kernels  22.7 us (97%)
  between operations  0.64 us (3%)
    pallas_call x1, Pallas kernels, local(): pl.pallas_call(lambda *refs: gather_kernel(counts, *refs), out_shape=(plt...  21.7 us
    pallas_call x1, Pallas kernels, local(): pl.pallas_call(backward_kernel, out_shape=(jax.ShapeDtypeStruct(slabs, f3...  0.96 us

profile of v7, /device:TPU:6, one launch (start us, length us, event | category | flops | bytes accessed | tf_op | source)
XLA Modules:
  0.0 23.3 jit_solution(5426555831544703011)
XLA Ops:
  0.6 21.7 %gather_cells.1 = (f32[27,2,8,128]{3,2,1,0:T(8,128)S(1)}, f32[27,2,8,128]{3,2,1,0:T(8,128)S(1)}, f32[2,8,128]{2,1,0:T(8,128)S(1)}, s32[2,8,128]{2,1,0:T(8,128)S(1)}) custom-call(f32[3,3,3,2,8,128]{5,4,3,2,1,0:T(8,128)} %bitcast.2, f32[3,3,3,2,8,128]{5,4,3,2,1,0:T(8,128)} %bitcast.3, f32[2,8,128]{2,1,0:T(8,128)} %refs_2_.1, s32[2,8,128]{2,1,0:T(8,128)} %refs_3_.1), custom_call_target="tpu_custom_call" | custom-call | tf_op jit(solution)/shard_map/gather_cells/pallas_call | solution.py:407
  22.3 1.0 %backward_cells.1 = (f32[27,2,8,128]{3,2,1,0:T(8,128)}, f32[2,8,128]{2,1,0:T(8,128)}) custom-call(f32[27,2,8,128]{3,2,1,0:T(8,128)S(1)} %get-tuple-element.6.final, f32[27,2,8,128]{3,2,1,0:T(8,128)S(1)} %get-tuple-element.7.pulled, f32[2,8,128]{2,1,0:T(8,128)S(1)} %get-tuple-element.8.design, s32[2,8,128]{2,1,0:T(8,128)S(1)} %get-tuple-element.9.node), custom_call_target="tpu_custom_call" | custom-call | tf_op jit(solution)/shard_map/backward_cells/pallas_call | solution.py:450
